TPU v7x, 768 devices: a whole 4x8x12 slice. The times are simulated.
768 devices in a mesh: band: 96 (over z, y), lev: 8 (over x, core).
Axes of the slice: x: 4, y: 8, z: 12, core: 2. Of those that a mesh axis runs over, the one named last changes fastest.
Arguments:
- spectra: bfloat16 [1344, 2, 120, 1280], P('band', None, 'lev'), may hold values from -6 to 6
- legendre: bfloat16 [1344, 1280, 192], P('band'), may hold values from -0.15625 to 0.15625
- slot_wave: int32 [1344], replicated, may hold values from -1 to 1279, as said below
- row_points: int32 [192], replicated, may hold values from 20 to 5136, as said below
- gauss_weight: float32 [192], replicated, may hold values from 0.5 to 2
- layer_depth: float32 [24], replicated, may hold values from 0.1 to 1
- mode_speed: float32 [120], P('lev'), may hold values from 0.5 to 8
Outputs:
- advanced: float32 [1344, 2, 120, 1280], P('band', None, 'lev')
Inputs may be any that keep to these rules, and one draw needn't show every extreme that they name: `slot_wave`: every wavenumber 0 to 1279 stands in exactly one slot. Slots 2k and 2k + 1 of one index of band hold a pair m and 1279 - m, or are both empty. `row_points`: rows 2k and 2k + 1 have 20 + 4 i and 20 + 4 (1279 - i) points for some i in 0 to 1279, in either order, so that together they have 4 * 1279 + 40 points.
All inputs are finite; a program needn't handle non-finite values.
Results may differ from a plain program's by a relative error of at most 0.0043.
Values may be sent and summed in bfloat16 or wider, within the bound.
A program may use at most 64 MiB of HBM per device.

v0:
```python
import functools

import jax
import jax.numpy as jnp
from jax import lax
from jax.experimental import pallas as pl
from jax.experimental.pallas import tpu as pltpu
from jax.sharding import PartitionSpec as P

TRUNC = 1279
FIELDS = 5
LEVELS = 24
FPAD = 16
LANES = 128
CHUNKS = 6
POINTS = CHUNKS * LANES
IMAGES = 8
JPAD = 8
F32 = jnp.float32
BF16 = jnp.bfloat16
I32 = jnp.int32
MESH = pl.DeviceIdType.MESH
NT = (((1,), (1,)), ((), ()))


def dot(a, b):
    return jnp.dot(a, b, preferred_element_type=F32)


def iota(shape, dim):
    return lax.broadcasted_iota(I32, shape, dim)


def lev_of_chunk(chunk):
    return chunk + chunk // 3


def quarter_turn_pair(quarters):
    nearest = jnp.round(quarters)
    u = quarters - nearest
    turn = nearest.astype(I32)
    u2 = u * u
    sin_u = u * (1.5707963 + u2 * (-0.6459640 + u2 * (0.07969087 + u2 * (-0.0046737664 + u2 * 0.00015148))))
    cos_u = 1.0 + u2 * (-1.2337005 + u2 * (0.25366950 + u2 * (-0.020863453 + u2 * 0.00091814)))
    odd = (turn & 1) == 1
    cos_v = jnp.where(odd, sin_u, cos_u)
    sin_v = jnp.where(odd, cos_u, sin_u)
    cos_v = jnp.where(((turn + 1) & 2) == 2, -cos_v, cos_v)
    sin_v = jnp.where((turn & 2) == 2, -sin_v, sin_v)
    return cos_v, sin_v


def base_points(p, first_points, second_points):
    first_count = first_points // 8 + 1
    second = p >= first_count
    index = jnp.where(second, p - first_count, p)
    length = jnp.where(second, second_points, first_points)
    return second, index, length, 8 * index <= length


def turn(wave, k):
    step = (jnp.maximum(wave, 0) * k) & 3
    real = jnp.where(step == 0, 1.0, jnp.where(step == 2, -1.0, 0.0))
    imag = jnp.where(step == 1, 1.0, jnp.where(step == 3, -1.0, 0.0))
    return real, imag


def round_kernel(
    nb,
    nl,
    wave_s,
    points_s,
    gauss_s,
    layer_s,
    wave_ref,
    spec_ref,
    leg_hbm,
    out_ref,
    leg_v,
    mix,
    fsend32,
    fsend,
    frecv,
    cos_v,
    sin_v,
    coef,
    rep,
    cos_w,
    sin_w,
    gsend,
    grecv,
    terms32,
    tsend,
    trecv,
    sums,
    diffs,
    ztab,
    back,
    bsend,
    leg_sem,
    send_sem,
    recv_sem,
):
    slots = leg_v.shape[0]
    pairs = slots // 2
    ndeg = leg_v.shape[2]
    nfld = spec_ref.shape[1]
    half = nb * JPAD
    qblock = min(16, nb)
    rows = qblock * JPAD
    blocks = nb // qblock
    band = lax.axis_index("band")
    lev = lax.axis_index("lev")

    copies = [pltpu.make_async_copy(leg_hbm.at[s], leg_v.at[s], leg_sem.at[s]) for s in range(slots)]
    for copy in copies:
        copy.start()

    barrier = pltpu.get_barrier_semaphore()

    @pl.loop(1, nb)
    def _(step):
        pl.semaphore_signal(barrier, inc=1, device_id=(lax.rem(band + step, nb), lev), device_id_type=MESH)

    @pl.loop(1, nl)
    def _(step):
        pl.semaphore_signal(barrier, inc=1, device_id=(band, lax.rem(lev + step, nl)), device_id_type=MESH)

    fsend32[...] = jnp.zeros_like(fsend32)
    degree = iota((2 * FPAD, ndeg), 1)
    blank = jnp.zeros((4 * FPAD, ndeg), BF16)
    fill = jnp.zeros((2 * FPAD - 2 * nfld, ndeg), BF16)
    second_lane = (iota((nb, LANES), 1) // (2 * FPAD)) % 2 == 1
    for j in range(pairs):
        parts = []
        for parity in range(2):
            s = 2 * j + parity
            wave = wave_s[band * slots + s]
            values = spec_ref[s].reshape(2 * nfld, ndeg)
            values = jnp.concatenate([values, fill], axis=0)
            first_degree = jnp.where(wave < 0, ndeg, wave)
            values = jnp.where(degree >= first_degree, values.astype(F32), 0.0).astype(BF16)
            whole = [values, values, blank] if parity == 0 else [blank, values, values]
            copies[s].wait()
            parts.append(
                lax.dot_general(leg_v[s], jnp.concatenate(whole, axis=0), NT, preferred_element_type=F32)
            )
        mix[...] = parts[0] + parts[1]
        first = mix[pl.ds(0, nb, stride=2), :]
        other = mix[pl.ds(1, nb, stride=2), :]
        fsend32[:, j, :] = jnp.where(second_lane, other, first)

    @pl.loop(0, blocks)
    def _(b):
        fsend[pl.ds(b * qblock, qblock)] = fsend32[pl.ds(b * qblock, qblock)].astype(BF16)

    pl.semaphore_wait(barrier, nb - 1 + nl - 1)

    @pl.loop(1, nb)
    def _(step):
        peer = lax.rem(band + step, nb)
        pltpu.make_async_remote_copy(
            src_ref=fsend.at[peer],
            dst_ref=frecv.at[band],
            send_sem=send_sem.at[0],
            recv_sem=recv_sem.at[0],
            device_id=(peer, lev),
            device_id_type=MESH,
        ).start()

    frecv[band] = fsend[band]

    first_points = points_s[2 * band]
    second_points = points_s[2 * band + 1]

    @pl.loop(0, POINTS // 16)
    def _(i):
        p = i * 16 + iota((16, LANES), 0)
        _, index, length, valid = base_points(p, first_points, second_points)
        length = length.astype(F32)
        inverse = 1.0 / length
        index = index.astype(F32)
        scale = 1.0 / jnp.sqrt(length)
        limit = jnp.where(valid, length - 1.0, -1.0)
        for lane in range(2 * half // rows):
            cut = pl.ds(lane * rows, rows)
            wave = wave_ref[:, cut].astype(F32)
            if rows < LANES:
                place = [v[:, :rows] for v in (index, inverse, length, scale, limit)]
            else:
                place = [index, inverse, length, scale, limit]
            at, inv, size, height, top = place
            product = wave * at
            residue = product - jnp.floor(product * inv) * size
            cos_p, sin_p = quarter_turn_pair(residue * (4.0 * inv))
            height = jnp.where((2.0 * wave <= top) & (wave >= 0.0), height, 0.0)
            cos_v[pl.ds(i * 16, 16), cut] = (cos_p * height).astype(BF16)
            sin_v[pl.ds(i * 16, 16), cut] = (sin_p * height).astype(BF16)

    lane_k = iota((rows, LANES), 1)
    flip = jnp.where((lane_k // 4) % 2 == 0, -1.0, 1.0)
    for b in range(2 * blocks):
        cut = pl.ds(b * rows, rows)
        column = jnp.broadcast_to(wave_ref[:, cut].astype(F32), (LANES, rows)).T.astype(I32)
        real, imag = turn(column, lane_k % 4)
        mult = jnp.where(column < 0, 0.0, jnp.where(column == 0, 1.0, 2.0))
        coef[0, cut] = real * mult
        coef[1, cut] = -imag * mult
        coef[2, cut] = flip * real * mult
        coef[3, cut] = flip * imag * mult
        row_re, row_im = turn(jnp.broadcast_to(wave_ref[:, cut], (4, rows)), iota((4, rows), 0))
        ztab[pl.ds(0, 4), cut] = row_re
        ztab[pl.ds(4, 4), cut] = -row_im
    source = iota((LANES, 2 * LANES), 0)
    target = iota((LANES, 2 * LANES), 1)
    wanted = (target // LANES) * (2 * FPAD) + (target % LANES) // IMAGES * 2
    for parity in range(2):
        for component in range(2):
            hit = source == wanted + parity * 4 * FPAD + component
            rep[2 * parity + component] = jnp.where(hit, 1.0, 0.0).astype(BF16)

    pltpu.make_async_copy(frecv.at[pl.ds(0, nb - 1)], frecv.at[pl.ds(0, nb - 1)], recv_sem.at[0]).wait()

    @pl.loop(0, blocks)
    def _(b):
        block = frecv[pl.ds(b * qblock, qblock)].reshape(rows, LANES)
        for parity in range(2):
            cut = pl.ds(pl.multiple_of(parity * half + b * rows, rows), rows)
            part_re = dot(block, rep[2 * parity])
            part_im = dot(block, rep[2 * parity + 1])
            for row in range(2):
                lanes = slice(row * LANES, row * LANES + LANES)
                re, im = part_re[:, lanes], part_im[:, lanes]
                cos_w[cut, lanes] = (coef[0, cut] * re + coef[1, cut] * im).astype(BF16)
                sin_w[cut, lanes] = (coef[2, cut] * im + coef[3, cut] * re).astype(BF16)

    @pl.loop(0, CHUNKS // 2)
    def _(c):
        cut = pl.ds(pl.multiple_of(c * 2 * LANES, 2 * LANES), 2 * LANES)
        values = dot(cos_v[cut, :], cos_w[...]) + dot(sin_v[cut, :], sin_w[...])
        for part in range(2):
            here = slice(part * LANES, part * LANES + LANES)
            p = (2 * c + part) * LANES + iota((LANES, LANES), 0)
            second, _, _, _ = base_points(p, first_points, second_points)
            chosen = jnp.where(second, values[here, LANES:], values[here, :LANES])
            gsend[2 * c + part] = chosen.T.astype(BF16).reshape(FPAD, IMAGES, LANES)

    for chunk in range(CHUNKS):
        target_lev = lev_of_chunk(chunk)

        @pl.when(lev != target_lev)
        def _():
            pltpu.make_async_remote_copy(
                src_ref=gsend.at[chunk],
                dst_ref=grecv.at[lev],
                send_sem=send_sem.at[1],
                recv_sem=recv_sem.at[1],
                device_id=(band, target_lev),
                device_id_type=MESH,
            ).start()

        @pl.when(lev == target_lev)
        def _():
            grecv[lev] = gsend[chunk]

    works = lax.rem(lev, 4) != 3

    @pl.when(works)
    def _():
        pltpu.make_async_copy(grecv.at[pl.ds(0, nl - 1)], grecv.at[pl.ds(0, nl - 1)], recv_sem.at[1]).wait()
        chunk = lev - lev // 4
        terms32[...] = jnp.zeros_like(terms32)

        def get(field, level):
            f = field * LEVELS + level
            return grecv[f // nfld, f % nfld].astype(F32)

        def put(field, level, value):
            f = field * LEVELS + level
            terms32[f // nfld, :, f % nfld, :] = value

        total = jnp.zeros((IMAGES, LANES), F32)
        for level in reversed(range(LEVELS)):
            wind_u, wind_v, temper = get(0, level), get(1, level), get(2, level)
            total = total + layer_s[level] * temper
            put(0, level, wind_u * temper)
            put(1, level, wind_v * temper)
            put(2, level, wind_u * get(3, level))
            put(3, level, wind_v * get(4, level))
            put(4, level, 0.5 * (wind_u * wind_u + wind_v * wind_v) + total)
        for target_lev in range(nl):
            tsend[target_lev] = terms32[target_lev].reshape(LANES, LANES).astype(BF16)

        @pl.loop(1, nl)
        def _(step):
            peer = lax.rem(lev + step, nl)
            pltpu.make_async_remote_copy(
                src_ref=tsend.at[peer],
                dst_ref=trecv.at[chunk],
                send_sem=send_sem.at[2],
                recv_sem=recv_sem.at[2],
                device_id=(band, peer),
                device_id_type=MESH,
            ).start()

        trecv[chunk] = tsend[lev]
        pltpu.make_async_copy(
            trecv.at[pl.ds(0, CHUNKS - 1)], trecv.at[pl.ds(0, CHUNKS - 1)], recv_sem.at[2]
        ).wait()

    @pl.when(jnp.logical_not(works))
    def _():
        pltpu.make_async_copy(trecv, trecv, recv_sem.at[2]).wait()

    for chunk in range(CHUNKS):
        p = chunk * LANES + iota((1, LANES), 1)
        second, index, length, valid = base_points(p, first_points, second_points)
        alone = (index == 0) | (8 * index == length)
        keep = jnp.where(valid, jnp.where(alone, 0.5, 1.0), 0.0)
        pieces = trecv[chunk].astype(F32)
        plus, minus = pieces[: 4 * FPAD], pieces[4 * FPAD :]
        lanes = slice(chunk * LANES, chunk * LANES + LANES)
        for row in range(2):
            kept = jnp.where(second, keep, 0.0) if row else jnp.where(second, 0.0, keep)
            to = slice(row * 4 * FPAD, (row + 1) * 4 * FPAD)
            sums[to, lanes] = ((plus + minus) * kept).astype(BF16)
            diffs[to, lanes] = ((plus - minus) * kept).astype(BF16)

    for b in range(blocks):
        for parity in range(2):
            cut = pl.ds(parity * half + b * rows, rows)
            cos_z = dot(sums[...], cos_v[:, cut])
            sin_z = dot(diffs[...], sin_v[:, cut])
            for row in range(2):
                re = jnp.zeros((FPAD, rows), F32)
                im = jnp.zeros((FPAD, rows), F32)
                for k in range(4):
                    at = (row * 4 + k) * FPAD
                    zr, zi = ztab[pl.ds(k, 1), cut], ztab[pl.ds(4 + k, 1), cut]
                    cz, sz = cos_z[at : at + FPAD], sin_z[at : at + FPAD]
                    re = re + zr * cz + zi * sz
                    im = im + zi * cz - zr * sz
                weight = gauss_s[2 * band + row]
                at = parity * 4 * FPAD + row * 2 * FPAD
                back[pl.ds(at, FPAD, stride=2), :] = re * weight
                back[pl.ds(at + 1, FPAD, stride=2), :] = im * weight
        bsend[pl.ds(b * qblock, qblock)] = back[...].T.astype(BF16).reshape(qblock, JPAD, LANES)

    @pl.loop(1, nb)
    def _(step):
        peer = lax.rem(band + step, nb)
        pltpu.make_async_remote_copy(
            src_ref=bsend.at[peer],
            dst_ref=out_ref.at[band],
            send_sem=send_sem.at[3],
            recv_sem=recv_sem.at[3],
            device_id=(peer, lev),
            device_id_type=MESH,
        ).start()

    out_ref[band] = bsend[band]
    pltpu.make_async_copy(out_ref.at[pl.ds(0, nb - 1)], out_ref.at[pl.ds(0, nb - 1)], recv_sem.at[3]).wait()

    pltpu.make_async_copy(fsend.at[pl.ds(0, nb - 1)], fsend.at[pl.ds(0, nb - 1)], send_sem.at[0]).wait()
    pltpu.make_async_copy(bsend.at[pl.ds(0, nb - 1)], bsend.at[pl.ds(0, nb - 1)], send_sem.at[3]).wait()

    @pl.when(works)
    def _():
        pltpu.make_async_copy(gsend.at[pl.ds(0, CHUNKS - 1)], gsend.at[pl.ds(0, CHUNKS - 1)], send_sem.at[1]).wait()
        pltpu.make_async_copy(tsend.at[pl.ds(0, nl - 1)], tsend.at[pl.ds(0, nl - 1)], send_sem.at[2]).wait()

    @pl.when(jnp.logical_not(works))
    def _():
        pltpu.make_async_copy(gsend, gsend, send_sem.at[1]).wait()


def update_kernel(nb, wave_s, wide_ref, arrived_ref, spec_ref, leg_ref, inverse_ref, out_ref, wide, mix, left):
    j = pl.program_id(0)
    band = lax.axis_index("band")
    ndeg = leg_ref.shape[2]
    nfld = spec_ref.shape[1]
    pairs = pl.num_programs(0)

    @pl.when(j == 0)
    def _():
        wide[...] = arrived_ref[...].astype(F32)

    mine = wide[:, j, :]
    mix[pl.ds(0, nb, stride=2), :] = mine
    mix[pl.ds(1, nb, stride=2), :] = mine
    nlat = mix.shape[0]
    fits = (iota((nlat, LANES), 0) % 2) == (iota((nlat, LANES), 1) // (2 * FPAD)) % 2
    turned = jnp.where(fits, mix[...], 0.0).T
    degree = iota((2 * nfld, ndeg), 1)
    for parity in range(2):
        at = parity * 4 * FPAD
        both = (turned[at : at + 2 * FPAD] + turned[at + 2 * FPAD : at + 4 * FPAD]).astype(BF16)
        tendency = dot(both, leg_ref[parity])[: 2 * nfld]
        wave = wave_s[band * 2 * pairs + 2 * j + parity]
        first_degree = jnp.where(wave < 0, ndeg, wave)
        values = spec_ref[parity].reshape(2 * nfld, ndeg).astype(F32)
        advanced = (values + tendency) * inverse_ref[...]
        advanced = jnp.where(degree >= first_degree, advanced, 0.0)
        out_ref[parity] = advanced.reshape(nfld, 2, ndeg)


def shards(spectra, legendre, slot_wave, row_points, gauss_weight, layer_depth, mode_speed):
    slots, _, nfld, ndeg = spectra.shape
    nb = lax.axis_size("band")
    nl = lax.axis_size("lev")
    nlat = legendre.shape[2]
    pairs = slots // 2
    half = nb * JPAD
    rows = min(16, nb) * JPAD
    wave = slot_wave.reshape(nb, pairs, 2).transpose(2, 0, 1)
    wave = jnp.pad(wave, ((0, 0), (0, 0), (0, JPAD - pairs)), constant_values=-1).reshape(1, 2 * half)
    spec_rows = spectra.transpose(0, 2, 1, 3)
    leg_rows = legendre.transpose(0, 2, 1)
    smem = pl.BlockSpec(memory_space=pltpu.SMEM)
    vmem = pl.BlockSpec(memory_space=pltpu.VMEM)
    arrived = pl.pallas_call(
        functools.partial(round_kernel, nb, nl),
        out_shape=jax.ShapeDtypeStruct((nb, JPAD, LANES), BF16),
        in_specs=[smem] * 4 + [vmem, vmem, pl.BlockSpec(memory_space=pl.ANY)],
        out_specs=vmem,
        scratch_shapes=[
            pltpu.VMEM((slots, nlat, ndeg), BF16),
            pltpu.VMEM((nlat, LANES), F32),
            pltpu.VMEM((nb, JPAD, LANES), F32),
            pltpu.VMEM((nb, JPAD, LANES), BF16),
            pltpu.VMEM((nb, JPAD, LANES), BF16),
            pltpu.VMEM((POINTS, 2 * half), BF16),
            pltpu.VMEM((POINTS, 2 * half), BF16),
            pltpu.VMEM((4, 2 * half, LANES), F32),
            pltpu.VMEM((4, LANES, 2 * LANES), BF16),
            pltpu.VMEM((2 * half, 2 * LANES), BF16),
            pltpu.VMEM((2 * half, 2 * LANES), BF16),
            pltpu.VMEM((CHUNKS, FPAD, IMAGES, LANES), BF16),
            pltpu.VMEM((nl, FPAD, IMAGES, LANES), BF16),
            pltpu.VMEM((nl, IMAGES, FPAD, LANES), F32),
            pltpu.VMEM((nl, LANES, LANES), BF16),
            pltpu.VMEM((CHUNKS, LANES, LANES), BF16),
            pltpu.VMEM((LANES, POINTS), BF16),
            pltpu.VMEM((LANES, POINTS), BF16),
            pltpu.VMEM((8, 2 * half), F32),
            pltpu.VMEM((LANES, rows), F32),
            pltpu.VMEM((nb, JPAD, LANES), BF16),
            pltpu.SemaphoreType.DMA((slots,)),
            pltpu.SemaphoreType.DMA((4,)),
            pltpu.SemaphoreType.DMA((4,)),
        ],
        compiler_params=pltpu.CompilerParams(
            collective_id=0, has_side_effects=True, vmem_limit_bytes=56 * 1024 * 1024
        ),
    )(slot_wave, row_points, gauss_weight, layer_depth, wave, spec_rows, leg_rows)

    degree = jnp.arange(ndeg, dtype=I32)
    helm = (degree * (degree + 1)).astype(F32) / float(TRUNC * (TRUNC + 1))
    inverse = 1.0 / (1.0 + helm[None, :] * jnp.repeat(mode_speed, 2)[:, None])
    out = pl.pallas_call(
        functools.partial(update_kernel, nb),
        grid=(pairs,),
        out_shape=jax.ShapeDtypeStruct((slots, nfld, 2, ndeg), F32),
        in_specs=[
            smem,
            smem,
            pl.BlockSpec((nb, JPAD, LANES), lambda j: (0, 0, 0)),
            pl.BlockSpec((2, nfld, 2, ndeg), lambda j: (j, 0, 0, 0)),
            pl.BlockSpec((2, nlat, ndeg), lambda j: (j, 0, 0)),
            pl.BlockSpec((2 * nfld, ndeg), lambda j: (0, 0)),
        ],
        out_specs=pl.BlockSpec((2, nfld, 2, ndeg), lambda j: (j, 0, 0, 0)),
        scratch_shapes=[
            pltpu.VMEM((nb, JPAD, LANES), F32),
            pltpu.VMEM((nlat, LANES), F32),
            pltpu.VMEM((8, LANES), F32),
        ],
    )(slot_wave, row_points, arrived, spec_rows, leg_rows, inverse)
    return out.transpose(0, 2, 1, 3)


def solution(mesh):
    return jax.shard_map(
        shards,
        mesh=mesh,
        in_specs=(P("band", None, "lev", None), P("band", None, None), P(), P(), P(), P(), P("lev")),
        out_specs=P("band", None, "lev", None),
        check_vma=False,
    )
```

profile of v0, /device:TPU:1, one launch (start us, length us, event | category | flops | bytes accessed | tf_op | source)
XLA Modules:
  0.0 76.3 jit_solution(6959354012873185940)
XLA Ops:
  0.0 0.7 broadcast_in_dim.4
  0.7 0.1 mul.24
  0.8 0.8 add_divide_fusion.inverse_ref
  1.6 0.9 %reshape.15 = s32[96,7,2]{2,1,0:T(8,128)S(1)} reshape(s32[1344]{0:T(1024)} %wave_s.3) | data formatting | bytes 10752 | tf_op jit(solution)/shard_map/reshape | solution.py:415
  2.5 0.7 copy.9
  3.2 0.7 reshape.16.wave_ref
  3.9 64.1 %shard_map.73.arrived_ref = bf16[96,8,128]{2,1,0:T(8,128)(2,1)} custom-call(s32[1344]{0:T(1024)} %wave_s.3, s32[192]{0:T(256)} %wide_ref.1, f32[192]{0:T(256)} %gauss_s.1, f32[24]{0:T(128)} %layer_s.1, s32[1,1536]{1,0:T(1,128)} %reshape.16.wave_ref, bf16[14,15,2,1280]{3,2,1,0:T(2,128)(2,1)} %bitcast.6, bf16[14,192,1280]{2,1,0:T(8,128)(2,1)} %bitcast.4), custom_call_target="tpu_custom_call" | custom-call | tf_op jit(solution)/shard_map/pallas_call | solution.py:421
  68.0 8.3 %shard_map.74 = f32[14,15,2,1280]{3,2,1,0:T(2,128)} custom-call(s32[1344]{0:T(1024)} %wave_s.3, s32[192]{0:T(256)} %wide_ref.1, bf16[96,8,128]{2,1,0:T(8,128)(2,1)} %shard_map.73.arrived_ref, bf16[14,15,2,1280]{3,2,1,0:T(2,128)(2,1)} %bitcast.7, bf16[14,192,1280]{2,1,0:T(8,128)(2,1)} %bitcast.5, f32[30,1280]{1,0:T(8,128)} %add_divide_fusion.inverse_ref), custom_call_target="tpu_custom_call" | custom-call | tf_op jit(solution)/shard_map/pallas_call | solution.py:460
  (2 shorter events, 0.0 us)
where the time goes:
time: 76.7 us; the launch traced here: 76.3 us
  Pallas kernels  72.4 us (94%)
  local copies, waits for them, and re-layouts  3.14 us (4%)
  other arithmetic  0.77 us (1%)
    pallas_call x1, Pallas kernels, shards(): pl.pallas_call(functools.partial(round_kernel, nb, nl), out_shape=jax.Sha...  64.1 us
    pallas_call x1, Pallas kernels, shards(): pl.pallas_call(functools.partial(update_kernel, nb), grid=(pairs,), out_s...  8.26 us

commit v1 on v0

v1 whole, which is shorter than its diff:
```python
import functools

import jax
import jax.numpy as jnp
from jax import lax
from jax.experimental import pallas as pl
from jax.experimental.pallas import tpu as pltpu
from jax.sharding import PartitionSpec as P

TRUNC = 1279
FIELDS = 5
LEVELS = 24
FPAD = 16
LANES = 128
CHUNKS = 6
POINTS = CHUNKS * LANES
IMAGES = 8
JPAD = 8
F32 = jnp.float32
BF16 = jnp.bfloat16
I32 = jnp.int32
MESH = pl.DeviceIdType.MESH
NT = (((1,), (1,)), ((), ()))


def dot(a, b):
    return jnp.dot(a, b, preferred_element_type=F32)


def iota(shape, dim):
    return lax.broadcasted_iota(I32, shape, dim)


def lev_of_chunk(chunk):
    return chunk + chunk // 3


def quarter_turn_pair(quarters):
    nearest = jnp.round(quarters)
    u = quarters - nearest
    turn = nearest.astype(I32)
    u2 = u * u
    sin_u = u * (1.5707963 + u2 * (-0.6459640 + u2 * (0.07969087 + u2 * (-0.0046737664 + u2 * 0.00015148))))
    cos_u = 1.0 + u2 * (-1.2337005 + u2 * (0.25366950 + u2 * (-0.020863453 + u2 * 0.00091814)))
    odd = (turn & 1) == 1
    cos_v = jnp.where(odd, sin_u, cos_u)
    sin_v = jnp.where(odd, cos_u, sin_u)
    cos_v = jnp.where(((turn + 1) & 2) == 2, -cos_v, cos_v)
    sin_v = jnp.where((turn & 2) == 2, -sin_v, sin_v)
    return cos_v, sin_v


def base_points(p, first_points, second_points):
    first_count = first_points // 8 + 1
    second = p >= first_count
    index = jnp.where(second, p - first_count, p)
    length = jnp.where(second, second_points, first_points)
    return second, index, length, 8 * index <= length


def turn(wave, k):
    step = (jnp.maximum(wave, 0) * k) & 3
    real = jnp.where(step == 0, 1.0, jnp.where(step == 2, -1.0, 0.0))
    imag = jnp.where(step == 1, 1.0, jnp.where(step == 3, -1.0, 0.0))
    return real, imag


def round_kernel(
    nb,
    nl,
    wave_s,
    points_s,
    gauss_s,
    layer_s,
    spec_hbm,
    leg_hbm,
    out_ref,
    values_hbm,
    spec_ref,
    values_v,
    leg_v,
    wave_col,
    wave_row,
    mix,
    fsend32,
    fsend,
    frecv,
    cos_v,
    sin_v,
    coef,
    rep,
    cos_w,
    sin_w,
    gsend,
    grecv,
    terms32,
    tsend,
    trecv,
    sums,
    diffs,
    ztab,
    back,
    bsend,
    spec_sem,
    own_sem,
    values_sem,
    leg_sem,
    send_sem,
    recv_sem,
):
    slots = leg_v.shape[0]
    pairs = slots // 2
    ndeg = leg_v.shape[2]
    nfld = spec_ref.shape[1]
    half = nb * JPAD
    qblock = min(16, nb)
    rows = qblock * JPAD
    blocks = nb // qblock
    band = lax.axis_index("band")
    lev = lax.axis_index("lev")

    barrier = pltpu.get_barrier_semaphore()
    far = nb // 2

    def ahead(offset):
        return lax.rem(band + offset, nb)

    def each_peer(act):
        act(ahead(far))

        @pl.loop(1, far)
        def _(step):
            act(ahead(far - step))
            act(ahead(far + step))

    each_peer(lambda peer: pl.semaphore_signal(barrier, inc=1, device_id=(peer, lev), device_id_type=MESH))

    @pl.loop(1, nl)
    def _(step):
        pl.semaphore_signal(barrier, inc=1, device_id=(band, lax.rem(lev + step, nl)), device_id_type=MESH)

    spec_copy = pltpu.make_async_copy(spec_hbm, spec_ref, spec_sem)
    spec_copy.start()
    copies = [pltpu.make_async_copy(leg_hbm.at[s], leg_v.at[s], leg_sem.at[s]) for s in range(slots)]
    for copy in copies:
        copy.start()

    fsend32[...] = jnp.zeros_like(fsend32)
    degree = iota((FPAD, ndeg), 1)
    blank = jnp.zeros((4 * FPAD, ndeg), BF16)
    fill = jnp.zeros((FPAD - nfld, ndeg), F32)
    second_lane = (iota((nb, LANES), 1) // (2 * FPAD)) % 2 == 1
    spec_copy.wait()
    for j in range(pairs):
        parts = []
        for parity in range(2):
            s = 2 * j + parity
            wave = wave_s[band * slots + s]
            first_degree = jnp.where(wave < 0, ndeg, wave)
            loaded = spec_ref[s].astype(F32)
            components = []
            for component in range(2):
                values = jnp.concatenate([loaded[:, component, :], fill], axis=0)
                components.append(jnp.where(degree >= first_degree, values, 0.0).astype(BF16))
            values_v[s] = jnp.concatenate(components, axis=0)
            values = values_v[s]
            whole = [values, values, blank] if parity == 0 else [blank, values, values]
            copies[s].wait()
            parts.append(
                lax.dot_general(leg_v[s], jnp.concatenate(whole, axis=0), NT, preferred_element_type=F32)
            )
        mix[...] = parts[0] + parts[1]
        first = mix[pl.ds(0, nb, stride=2), :]
        other = mix[pl.ds(1, nb, stride=2), :]
        fsend32[:, j, :] = jnp.where(second_lane, other, first)

    values_copy = pltpu.make_async_copy(values_v, values_hbm, values_sem)
    values_copy.start()

    @pl.loop(0, blocks)
    def _(b):
        fsend[pl.ds(b * qblock, qblock)] = fsend32[pl.ds(b * qblock, qblock)].astype(BF16)

    pl.semaphore_wait(barrier, nb - 1 + nl - 1)

    def send_coefficients(peer):
        pltpu.make_async_remote_copy(
            src_ref=fsend.at[peer],
            dst_ref=frecv.at[band],
            send_sem=send_sem.at[0],
            recv_sem=recv_sem.at[0],
            device_id=(peer, lev),
            device_id_type=MESH,
        ).start()

    each_peer(send_coefficients)
    frecv[band] = fsend[band]

    first_points = points_s[2 * band]
    second_points = points_s[2 * band + 1]

    row8 = iota((JPAD, LANES), 0)

    @pl.loop(0, nb)
    def _(q):
        for parity in range(2):
            column = jnp.full((JPAD, LANES), -1, I32)
            for j in range(pairs):
                column = jnp.where(row8 == j, wave_s[q * slots + 2 * j + parity], column)
            wave_col[pl.ds(pl.multiple_of(parity * half + q * JPAD, JPAD), JPAD), :] = column

    lane_k = iota((rows, LANES), 1)
    flip = jnp.where((lane_k // 4) % 2 == 0, -1.0, 1.0)
    for b in range(2 * blocks):
        cut = pl.ds(b * rows, rows)
        column = wave_col[cut, :]
        real, imag = turn(column, lane_k % 4)
        mult = jnp.where(column < 0, 0.0, jnp.where(column == 0, 1.0, 2.0))
        coef[0, cut] = real * mult
        coef[1, cut] = -imag * mult
        coef[2, cut] = flip * real * mult
        coef[3, cut] = flip * imag * mult
        turned = column.astype(F32).T[:16]
        wave_row[:, cut] = turned
        row_re, row_im = turn(turned[:8].astype(I32), iota((8, rows), 0) % 4)
        ztab[:, cut] = jnp.where(iota((8, rows), 0) < 4, row_re, -row_im)

    @pl.loop(0, POINTS // 16)
    def _(i):
        p = i * 16 + iota((16, rows), 0)
        _, index, length, valid = base_points(p, first_points, second_points)
        length = length.astype(F32)
        inverse = 1.0 / length
        index = index.astype(F32)
        scale = 1.0 / jnp.sqrt(length)
        limit = jnp.where(valid, length - 1.0, -1.0)

        def angle(wave):
            product = wave * index
            residue = product - jnp.floor(product * inverse) * length
            return quarter_turn_pair(residue * (4.0 * inverse))

        whole_cos, whole_sin = angle(float(TRUNC))
        here = pl.ds(pl.multiple_of(i * 16, 16), 16)
        for lane in range(blocks):
            cut = pl.ds(lane * rows, rows)
            wave = wave_row[:, cut]
            cos_p, sin_p = angle(wave)
            height = jnp.where((2.0 * wave <= limit) & (wave >= 0.0), scale, 0.0)
            cos_v[here, cut] = (cos_p * height).astype(BF16)
            sin_v[here, cut] = (sin_p * height).astype(BF16)
            cut = pl.ds(half + lane * rows, rows)
            wave = wave_row[:, cut]
            height = jnp.where((2.0 * wave <= limit) & (wave >= 0.0), scale, 0.0)
            cos_v[here, cut] = ((whole_cos * cos_p + whole_sin * sin_p) * height).astype(BF16)
            sin_v[here, cut] = ((whole_sin * cos_p - whole_cos * sin_p) * height).astype(BF16)

    source = iota((LANES, 2 * LANES), 0)
    target = iota((LANES, 2 * LANES), 1)
    wanted = (target // LANES) * (2 * FPAD) + (target % LANES) // IMAGES
    for parity in range(2):
        for component in range(2):
            hit = source == wanted + parity * 4 * FPAD + component * FPAD
            rep[2 * parity + component] = jnp.where(hit, 1.0, 0.0).astype(BF16)

    pltpu.make_async_copy(frecv.at[pl.ds(0, nb - 1)], frecv.at[pl.ds(0, nb - 1)], recv_sem.at[0]).wait()

    @pl.loop(0, blocks)
    def _(b):
        block = frecv[pl.ds(b * qblock, qblock)].reshape(rows, LANES)
        for parity in range(2):
            cut = pl.ds(pl.multiple_of(parity * half + b * rows, rows), rows)
            part_re = dot(block, rep[2 * parity])
            part_im = dot(block, rep[2 * parity + 1])
            for row in range(2):
                lanes = slice(row * LANES, row * LANES + LANES)
                re, im = part_re[:, lanes], part_im[:, lanes]
                cos_w[cut, lanes] = (coef[0, cut] * re + coef[1, cut] * im).astype(BF16)
                sin_w[cut, lanes] = (coef[2, cut] * im + coef[3, cut] * re).astype(BF16)

    def send_points(chunk):
        target_lev = lev_of_chunk(chunk)

        @pl.when(lev != target_lev)
        def _():
            pltpu.make_async_remote_copy(
                src_ref=gsend.at[chunk, pl.ds(0, nfld)],
                dst_ref=grecv.at[lev, pl.ds(0, nfld)],
                send_sem=send_sem.at[1],
                recv_sem=recv_sem.at[1],
                device_id=(band, target_lev),
                device_id_type=MESH,
            ).start()

        @pl.when(lev == target_lev)
        def _():
            grecv[lev] = gsend[chunk]

    for c in range(CHUNKS // 2):
        cut = slice(c * 2 * LANES, (c + 1) * 2 * LANES)
        values = dot(cos_v[cut, :], cos_w[...]) + dot(sin_v[cut, :], sin_w[...])
        for part in range(2):
            here = slice(part * LANES, part * LANES + LANES)
            p = (2 * c + part) * LANES + iota((LANES, LANES), 0)
            second, _, _, _ = base_points(p, first_points, second_points)
            chosen = jnp.where(second, values[here, LANES:], values[here, :LANES])
            gsend[2 * c + part] = chosen.T.astype(BF16).reshape(FPAD, IMAGES, LANES)
            send_points(2 * c + part)

    works = lax.rem(lev, 4) != 3

    @pl.when(works)
    def _():
        others = grecv.at[pl.ds(0, nl - 1), pl.ds(0, nfld)]
        pltpu.make_async_copy(others, others, recv_sem.at[1]).wait()
        chunk = lev - lev // 4
        terms32[...] = jnp.zeros_like(terms32)

        def get(field, level):
            f = field * LEVELS + level
            return grecv[f // nfld, f % nfld].astype(F32)

        def put(field, level, value):
            f = field * LEVELS + level
            terms32[f // nfld, :, f % nfld, :] = value

        total = jnp.zeros((IMAGES, LANES), F32)
        for level in reversed(range(LEVELS)):
            wind_u, wind_v, temper = get(0, level), get(1, level), get(2, level)
            total = total + layer_s[level] * temper
            put(0, level, wind_u * temper)
            put(1, level, wind_v * temper)
            put(2, level, wind_u * get(3, level))
            put(3, level, wind_v * get(4, level))
            put(4, level, 0.5 * (wind_u * wind_u + wind_v * wind_v) + total)
        for target_lev in range(nl):
            tsend[target_lev] = terms32[target_lev].reshape(LANES, LANES).astype(BF16)

        @pl.loop(1, nl)
        def _(step):
            peer = lax.rem(lev + step, nl)
            pltpu.make_async_remote_copy(
                src_ref=tsend.at[peer],
                dst_ref=trecv.at[chunk],
                send_sem=send_sem.at[2],
                recv_sem=recv_sem.at[2],
                device_id=(band, peer),
                device_id_type=MESH,
            ).start()

        trecv[chunk] = tsend[lev]
        pltpu.make_async_copy(
            trecv.at[pl.ds(0, CHUNKS - 1)], trecv.at[pl.ds(0, CHUNKS - 1)], recv_sem.at[2]
        ).wait()

    @pl.when(jnp.logical_not(works))
    def _():
        pltpu.make_async_copy(trecv, trecv, recv_sem.at[2]).wait()

    for chunk in range(CHUNKS):
        p = chunk * LANES + iota((1, LANES), 1)
        second, index, length, valid = base_points(p, first_points, second_points)
        alone = (index == 0) | (8 * index == length)
        keep = jnp.where(valid, jnp.where(alone, 0.5, 1.0), 0.0)
        pieces = trecv[chunk].astype(F32)
        plus, minus = pieces[: 4 * FPAD], pieces[4 * FPAD :]
        lanes = slice(chunk * LANES, chunk * LANES + LANES)
        for row in range(2):
            kept = jnp.where(second, keep, 0.0) if row else jnp.where(second, 0.0, keep)
            to = slice(row * 4 * FPAD, (row + 1) * 4 * FPAD)
            sums[to, lanes] = ((plus + minus) * kept).astype(BF16)
            diffs[to, lanes] = ((plus - minus) * kept).astype(BF16)

    home = band // qblock
    order = sorted(range(blocks), key=lambda away: -min(away, blocks - away))
    for away in order:
        b = lax.rem(home + away, blocks)
        cuts = [pl.ds(pl.multiple_of(parity * half + b * rows, rows), rows) for parity in range(2)]

        def both(ref, at):
            return jnp.concatenate([ref[at, cut] for cut in cuts], axis=1)

        cos_z = dot(sums[...], both(cos_v, slice(None)))
        sin_z = dot(diffs[...], both(sin_v, slice(None)))
        for row in range(2):
            re = jnp.zeros((FPAD, 2 * rows), F32)
            im = jnp.zeros((FPAD, 2 * rows), F32)
            for k in range(4):
                at = (row * 4 + k) * FPAD
                zr, zi = both(ztab, pl.ds(k, 1)), both(ztab, pl.ds(4 + k, 1))
                cz, sz = cos_z[at : at + FPAD], sin_z[at : at + FPAD]
                re = re + zr * cz + zi * sz
                im = im + zi * cz - zr * sz
            weight = gauss_s[2 * band + row]
            for parity in range(2):
                at = parity * 4 * FPAD + row * 2 * FPAD
                lanes = slice(parity * rows, (parity + 1) * rows)
                back[pl.ds(at, FPAD), :] = re[:, lanes] * weight
                back[pl.ds(at + FPAD, FPAD), :] = im[:, lanes] * weight
        bsend[pl.ds(b * qblock, qblock)] = back[...].T.astype(BF16).reshape(qblock, JPAD, LANES)

        @pl.loop(0, qblock)
        def _(t):
            peer = b * qblock + t

            @pl.when(peer != band)
            def _():
                pltpu.make_async_remote_copy(
                    src_ref=bsend.at[peer],
                    dst_ref=out_ref.at[band],
                    send_sem=send_sem.at[3],
                    recv_sem=recv_sem.at[3],
                    device_id=(peer, lev),
                    device_id_type=MESH,
                ).start()

    own_copy = pltpu.make_async_copy(bsend.at[band], out_ref.at[band], own_sem)
    own_copy.start()
    own_copy.wait()
    values_copy.wait()
    pltpu.make_async_copy(out_ref.at[pl.ds(0, nb - 1)], out_ref.at[pl.ds(0, nb - 1)], recv_sem.at[3]).wait()

    pltpu.make_async_copy(fsend.at[pl.ds(0, nb - 1)], fsend.at[pl.ds(0, nb - 1)], send_sem.at[0]).wait()
    pltpu.make_async_copy(bsend.at[pl.ds(0, nb - 1)], bsend.at[pl.ds(0, nb - 1)], send_sem.at[3]).wait()

    @pl.when(works)
    def _():
        others = gsend.at[pl.ds(0, CHUNKS - 1), pl.ds(0, nfld)]
        pltpu.make_async_copy(others, others, send_sem.at[1]).wait()
        pltpu.make_async_copy(tsend.at[pl.ds(0, nl - 1)], tsend.at[pl.ds(0, nl - 1)], send_sem.at[2]).wait()

    @pl.when(jnp.logical_not(works))
    def _():
        others = gsend.at[:, pl.ds(0, nfld)]
        pltpu.make_async_copy(others, others, send_sem.at[1]).wait()


def update_kernel(
    nb, wave_s, speed_s, arrived_hbm, values_hbm, leg_hbm, out_hbm, arrived, values_v, leg_v, out_v, inverse, wide, mix, turned, sems, leg_sem, out_sem
):
    band = lax.axis_index("band")
    slots, nlat, ndeg = leg_v.shape
    nfld = speed_s.shape[0]
    pairs = slots // 2
    cuts = 5
    width = ndeg // cuts
    lanes = min(LANES, width)
    tiles = width // lanes
    per_field = 2 * cuts * tiles
    waves = [wave_s[band * slots + s] for s in range(slots)]
    firsts = [jnp.where(wave < 0, ndeg, wave) for wave in waves]

    def piece(j, t):
        start = jnp.maximum(waves[2 * j], 0) // width
        later = t >= cuts - start
        return jnp.where(later, 1, 0), jnp.where(later, t - 1, start + t)

    def leg_copy(j, t):
        parity, block = piece(j, t)
        cut = pl.ds(pl.multiple_of(block * width, width), width)
        slot = 2 * j + parity
        return pltpu.make_async_copy(leg_hbm.at[slot, :, cut], leg_v.at[slot, :, cut], leg_sem.at[j])

    def values_copy(j):
        cut = pl.ds(2 * j, 2)
        return pltpu.make_async_copy(values_hbm.at[cut], values_v.at[cut], sems.at[1 + j])

    arrived_copy = pltpu.make_async_copy(arrived_hbm, arrived, sems.at[0])
    arrived_copy.start()
    for j in range(pairs):
        values_copy(j).start()
        for t in range(cuts + 1):
            leg_copy(j, t).start()

    field = iota((FPAD, lanes), 0)
    speed = jnp.zeros((FPAD, lanes), F32)
    for f in range(nfld):
        speed = jnp.where(field == f, speed_s[f], speed)
    for at in range(0, ndeg, lanes):
        n = at + iota((FPAD, lanes), 1)
        helm = (n * (n + 1)).astype(F32) / float(TRUNC * (TRUNC + 1))
        inverse[:, at : at + lanes] = 1.0 / (1.0 + helm * speed)
    out_v[...] = jnp.zeros_like(out_v)
    fits = (iota((nlat, LANES), 0) % 2) == (iota((nlat, LANES), 1) // (2 * FPAD)) % 2
    degree = iota((FPAD, width), 1)
    arrived_copy.wait()
    wide[...] = arrived[...].astype(F32)
    for j in range(pairs):
        mine = wide[:, j, :]
        mix[pl.ds(0, nb, stride=2), :] = mine
        mix[pl.ds(1, nb, stride=2), :] = mine
        flat = jnp.where(fits, mix[...], 0.0).T
        for parity in range(2):
            at = parity * 4 * FPAD
            turned[2 * j + parity] = (flat[at : at + 2 * FPAD] + flat[at + 2 * FPAD : at + 4 * FPAD]).astype(BF16)

    for j in range(pairs):
        values_copy(j).wait()
        for t in range(cuts + 1):
            leg_copy(j, t).wait()
        for t in range(cuts + 1):
            parity, block = piece(j, t)
            slot = 2 * j + parity
            first_degree = jnp.where(parity == 0, firsts[2 * j], firsts[2 * j + 1])
            cut = pl.ds(pl.multiple_of(block * width, width), width)
            tendency = dot(turned[slot], leg_v[slot, :, cut])
            sum_here = values_v[slot, :, cut].astype(F32) + tendency
            live = degree + block * width >= first_degree
            for component in range(2):
                part = sum_here[component * FPAD : (component + 1) * FPAD] * inverse[:, cut]
                part = jnp.where(live, part, 0.0)
                for tile in range(tiles):
                    row = slot * nfld * per_field + (block * tiles + tile) * 2 + component
                    out_v[pl.ds(row, nfld, stride=per_field), :] = part[:nfld, tile * lanes : (tile + 1) * lanes]
        here = pl.ds(2 * j * nfld * per_field, 2 * nfld * per_field)
        pltpu.make_async_copy(out_v.at[here], out_hbm.at[here], out_sem.at[j]).start()
    for j in range(pairs):
        here = pl.ds(2 * j * nfld * per_field, 2 * nfld * per_field)
        pltpu.make_async_copy(out_v.at[here], out_hbm.at[here], out_sem.at[j]).wait()


def shards(spectra, legendre, slot_wave, row_points, gauss_weight, layer_depth, mode_speed):
    slots, _, nfld, ndeg = spectra.shape
    nb = lax.axis_size("band")
    nl = lax.axis_size("lev")
    nlat = legendre.shape[2]
    pairs = slots // 2
    half = nb * JPAD
    rows = min(16, nb) * JPAD
    spec_rows = spectra.transpose(0, 2, 1, 3)
    leg_rows = legendre.transpose(0, 2, 1)
    smem = pl.BlockSpec(memory_space=pltpu.SMEM)
    anywhere = pl.BlockSpec(memory_space=pl.ANY)
    arrived, values = pl.pallas_call(
        functools.partial(round_kernel, nb, nl),
        out_shape=(
            jax.ShapeDtypeStruct((nb, JPAD, LANES), BF16),
            jax.ShapeDtypeStruct((slots, 2 * FPAD, ndeg), BF16),
        ),
        in_specs=[smem] * 4 + [anywhere, anywhere],
        out_specs=(anywhere, anywhere),
        scratch_shapes=[
            pltpu.VMEM((slots, nfld, 2, ndeg), BF16),
            pltpu.VMEM((slots, 2 * FPAD, ndeg), BF16),
            pltpu.VMEM((slots, nlat, ndeg), BF16),
            pltpu.VMEM((2 * half, LANES), I32),
            pltpu.VMEM((16, 2 * half), F32),
            pltpu.VMEM((nlat, LANES), F32),
            pltpu.VMEM((nb, JPAD, LANES), F32),
            pltpu.VMEM((nb, JPAD, LANES), BF16),
            pltpu.VMEM((nb, JPAD, LANES), BF16),
            pltpu.VMEM((POINTS, 2 * half), BF16),
            pltpu.VMEM((POINTS, 2 * half), BF16),
            pltpu.VMEM((4, 2 * half, LANES), F32),
            pltpu.VMEM((4, LANES, 2 * LANES), BF16),
            pltpu.VMEM((2 * half, 2 * LANES), BF16),
            pltpu.VMEM((2 * half, 2 * LANES), BF16),
            pltpu.VMEM((CHUNKS, FPAD, IMAGES, LANES), BF16),
            pltpu.VMEM((nl, FPAD, IMAGES, LANES), BF16),
            pltpu.VMEM((nl, IMAGES, FPAD, LANES), F32),
            pltpu.VMEM((nl, LANES, LANES), BF16),
            pltpu.VMEM((CHUNKS, LANES, LANES), BF16),
            pltpu.VMEM((LANES, POINTS), BF16),
            pltpu.VMEM((LANES, POINTS), BF16),
            pltpu.VMEM((8, 2 * half), F32),
            pltpu.VMEM((LANES, rows), F32),
            pltpu.VMEM((nb, JPAD, LANES), BF16),
            pltpu.SemaphoreType.DMA,
            pltpu.SemaphoreType.DMA,
            pltpu.SemaphoreType.DMA,
            pltpu.SemaphoreType.DMA((slots,)),
            pltpu.SemaphoreType.DMA((4,)),
            pltpu.SemaphoreType.DMA((4,)),
        ],
        compiler_params=pltpu.CompilerParams(
            collective_id=0, has_side_effects=True, vmem_limit_bytes=56 * 1024 * 1024
        ),
    )(slot_wave, row_points, gauss_weight, layer_depth, spec_rows, leg_rows)

    lanes = min(LANES, ndeg // 5)
    tiles = ndeg // lanes
    out = pl.pallas_call(
        functools.partial(update_kernel, nb),
        out_shape=jax.ShapeDtypeStruct((slots * nfld * tiles * 2, lanes), F32),
        in_specs=[smem, smem, anywhere, anywhere, anywhere],
        out_specs=anywhere,
        scratch_shapes=[
            pltpu.VMEM((nb, JPAD, LANES), BF16),
            pltpu.VMEM((slots, 2 * FPAD, ndeg), BF16),
            pltpu.VMEM((slots, nlat, ndeg), BF16),
            pltpu.VMEM((slots * nfld * tiles * 2, lanes), F32),
            pltpu.VMEM((FPAD, ndeg), F32),
            pltpu.VMEM((nb, JPAD, LANES), F32),
            pltpu.VMEM((nlat, LANES), F32),
            pltpu.VMEM((slots, 2 * FPAD, nlat), BF16),
            pltpu.SemaphoreType.DMA((1 + pairs,)),
            pltpu.SemaphoreType.DMA((pairs,)),
            pltpu.SemaphoreType.DMA((pairs,)),
        ],
        compiler_params=pltpu.CompilerParams(vmem_limit_bytes=56 * 1024 * 1024),
    )(slot_wave, mode_speed, arrived, values, leg_rows)
    out = out.reshape(slots, nfld, tiles, 2, lanes).transpose(0, 1, 3, 2, 4)
    return out.reshape(slots, nfld, 2, ndeg).transpose(0, 2, 1, 3)


def solution(mesh):
    return jax.shard_map(
        shards,
        mesh=mesh,
        in_specs=(P("band", None, "lev", None), P("band", None, None), P(), P(), P(), P(), P("lev")),
        out_specs=P("band", None, "lev", None),
        check_vma=False,
    )
```

time: 76.7 us -> 67.8 us (0.88)
  Pallas kernels: 72.4 us -> 67.6 us
  local copies, waits for them, and re-layouts: 3.14 us -> 0 us
  other arithmetic: 0.77 us -> 0 us
    pallas_call x2, Pallas kernels: 72.4 us -> 67.6 us  [the longest x1 61.8 us: shards(): pl.pallas_call(functools.partial(round_kernel, nb, nl), out_shape=(jax.Sh...]
    reshape x2 -> x0, local copies, waits for them, and re-layouts: 1.6 us -> none  [the longest x1 0.89 us: shards(): wave = slot_wave.reshape(nb, pairs, 2).transpose(2, 0, 1)]
where the time goes in v1:
time: 67.8 us; the launch traced here: 67.6 us
  Pallas kernels  67.6 us (100%)
    pallas_call x1, Pallas kernels, shards(): pl.pallas_call(functools.partial(round_kernel, nb, nl), out_shape=(jax.Sh...  61.8 us
    pallas_call x1, Pallas kernels, shards(): pl.pallas_call(functools.partial(update_kernel, nb), out_shape=jax.ShapeD...  5.8 us

profile of v1, /device:TPU:1, one launch (start us, length us, event | category | flops | bytes accessed | tf_op | source)
XLA Modules:
  0.0 67.6 jit_solution(657504088808945270)
XLA Ops:
  0.0 61.8 %shard_map.73 = (bf16[96,8,128]{2,1,0:T(8,128)(2,1)}, bf16[14,32,1280]{2,1,0:T(8,128)(2,1)}) custom-call(s32[1344]{0:T(1024)} %wave_s.3, s32[192]{0:T(256)} %points_s.1, f32[192]{0:T(256)} %gauss_s.1, f32[24]{0:T(128)} %layer_s.1, bf16[14,15,2,1280]{3,2,1,0:T(2,128)(2,1)} %bitcast.11, bf16[14,192,1280]{2,1,0:T(8,128)(2,1)} %bitcast.9), custom_call_target="tpu_custom_call" | custom-call | tf_op jit(solution)/shard_map/pallas_call | solution.py:534
  61.8 5.8 %shard_map.74 = f32[4200,128]{1,0:T(8,128)} custom-call(s32[1344]{0:T(1024)} %wave_s.3, f32[15]{0:T(128)} %speed_s.1, bf16[96,8,128]{2,1,0:T(8,128)(2,1)} %get-tuple-element.7.arrived_hbm, bf16[14,32,1280]{2,1,0:T(8,128)(2,1)} %get-tuple-element.8.values_hbm, bf16[14,192,1280]{2,1,0:T(8,128)(2,1)} %bitcast.10), custom_call_target="tpu_custom_call" | custom-call | tf_op jit(solution)/shard_map/pallas_call | solution.py:582

commit v2 on v1

--- a/solution.py
+++ b/solution.py
@@ -35,19 +35,11 @@
     return chunk + chunk // 3
 
 
-def quarter_turn_pair(quarters):
-    nearest = jnp.round(quarters)
-    u = quarters - nearest
-    turn = nearest.astype(I32)
+def half_turn_pair(u):
     u2 = u * u
-    sin_u = u * (1.5707963 + u2 * (-0.6459640 + u2 * (0.07969087 + u2 * (-0.0046737664 + u2 * 0.00015148))))
-    cos_u = 1.0 + u2 * (-1.2337005 + u2 * (0.25366950 + u2 * (-0.020863453 + u2 * 0.00091814)))
-    odd = (turn & 1) == 1
-    cos_v = jnp.where(odd, sin_u, cos_u)
-    sin_v = jnp.where(odd, cos_u, sin_u)
-    cos_v = jnp.where(((turn + 1) & 2) == 2, -cos_v, cos_v)
-    sin_v = jnp.where((turn & 2) == 2, -sin_v, sin_v)
-    return cos_v, sin_v
+    sin_u = u * (3.14158202 + u2 * (-5.16714279 + u2 * (2.54189895 + u2 * -0.554635995)))
+    cos_u = 1.0 + u2 * (-4.93479552 + u2 * (4.05845134 + u2 * (-1.33209382 + u2 * 0.220080563)))
+    return cos_u, sin_u
 
 
 def base_points(p, first_points, second_points):
@@ -146,9 +138,9 @@
         copy.start()
 
     fsend32[...] = jnp.zeros_like(fsend32)
-    degree = iota((FPAD, ndeg), 1)
+    degree = iota((2 * FPAD, ndeg), 1)
     blank = jnp.zeros((4 * FPAD, ndeg), BF16)
-    fill = jnp.zeros((FPAD - nfld, ndeg), F32)
+    fill = jnp.zeros((2 * FPAD - 2 * nfld, ndeg), BF16)
     second_lane = (iota((nb, LANES), 1) // (2 * FPAD)) % 2 == 1
     spec_copy.wait()
     for j in range(pairs):
@@ -156,14 +148,10 @@
         for parity in range(2):
             s = 2 * j + parity
             wave = wave_s[band * slots + s]
+            values = spec_ref[s].reshape(2 * nfld, ndeg)
+            values = jnp.concatenate([values, fill], axis=0)
             first_degree = jnp.where(wave < 0, ndeg, wave)
-            loaded = spec_ref[s].astype(F32)
-            components = []
-            for component in range(2):
-                values = jnp.concatenate([loaded[:, component, :], fill], axis=0)
-                components.append(jnp.where(degree >= first_degree, values, 0.0).astype(BF16))
-            values_v[s] = jnp.concatenate(components, axis=0)
-            values = values_v[s]
+            values = jnp.where(degree >= first_degree, values.astype(F32), 0.0).astype(BF16)
             whole = [values, values, blank] if parity == 0 else [blank, values, values]
             copies[s].wait()
             parts.append(
@@ -173,9 +161,6 @@
         first = mix[pl.ds(0, nb, stride=2), :]
         other = mix[pl.ds(1, nb, stride=2), :]
         fsend32[:, j, :] = jnp.where(second_lane, other, first)
-
-    values_copy = pltpu.make_async_copy(values_v, values_hbm, values_sem)
-    values_copy.start()
 
     @pl.loop(0, blocks)
     def _(b):
@@ -221,7 +206,7 @@
         coef[2, cut] = flip * real * mult
         coef[3, cut] = flip * imag * mult
         turned = column.astype(F32).T[:16]
-        wave_row[:, cut] = turned
+        wave_row[:, cut] = jnp.where(turned < 0.0, 1.0e5, turned)
         row_re, row_im = turn(turned[:8].astype(I32), iota((8, rows), 0) % 4)
         ztab[:, cut] = jnp.where(iota((8, rows), 0) < 4, row_re, -row_im)
 
@@ -231,36 +216,39 @@
         _, index, length, valid = base_points(p, first_points, second_points)
         length = length.astype(F32)
         inverse = 1.0 / length
-        index = index.astype(F32)
+        doubled = 2.0 * index.astype(F32)
         scale = 1.0 / jnp.sqrt(length)
-        limit = jnp.where(valid, length - 1.0, -1.0)
+        limit = jnp.where(valid, 0.5 * (length - 1.0), -1.0)
 
         def angle(wave):
-            product = wave * index
-            residue = product - jnp.floor(product * inverse) * length
-            return quarter_turn_pair(residue * (4.0 * inverse))
-
-        whole_cos, whole_sin = angle(float(TRUNC))
+            product = wave * doubled
+            nearest = jnp.round(product * inverse)
+            cos_u, sin_u = half_turn_pair((product - nearest * length) * inverse)
+            return cos_u, sin_u, (nearest.astype(I32) & 1) == 1
+
+        whole_cos, whole_sin, odd = angle(float(TRUNC))
+        whole_cos = jnp.where(odd, -whole_cos, whole_cos)
+        whole_sin = jnp.where(odd, -whole_sin, whole_sin)
         here = pl.ds(pl.multiple_of(i * 16, 16), 16)
         for lane in range(blocks):
             cut = pl.ds(lane * rows, rows)
             wave = wave_row[:, cut]
-            cos_p, sin_p = angle(wave)
-            height = jnp.where((2.0 * wave <= limit) & (wave >= 0.0), scale, 0.0)
+            cos_p, sin_p, odd = angle(wave)
+            signed = jnp.where(odd, -scale, scale)
+            height = jnp.where(wave <= limit, signed, 0.0)
             cos_v[here, cut] = (cos_p * height).astype(BF16)
             sin_v[here, cut] = (sin_p * height).astype(BF16)
             cut = pl.ds(half + lane * rows, rows)
-            wave = wave_row[:, cut]
-            height = jnp.where((2.0 * wave <= limit) & (wave >= 0.0), scale, 0.0)
+            height = jnp.where(wave_row[:, cut] <= limit, signed, 0.0)
             cos_v[here, cut] = ((whole_cos * cos_p + whole_sin * sin_p) * height).astype(BF16)
             sin_v[here, cut] = ((whole_sin * cos_p - whole_cos * sin_p) * height).astype(BF16)
 
     source = iota((LANES, 2 * LANES), 0)
     target = iota((LANES, 2 * LANES), 1)
-    wanted = (target // LANES) * (2 * FPAD) + (target % LANES) // IMAGES
+    wanted = (target // LANES) * (2 * FPAD) + (target % LANES) // IMAGES * 2
     for parity in range(2):
         for component in range(2):
-            hit = source == wanted + parity * 4 * FPAD + component * FPAD
+            hit = source == wanted + parity * 4 * FPAD + component
             rep[2 * parity + component] = jnp.where(hit, 1.0, 0.0).astype(BF16)
 
     pltpu.make_async_copy(frecv.at[pl.ds(0, nb - 1)], frecv.at[pl.ds(0, nb - 1)], recv_sem.at[0]).wait()
@@ -416,6 +404,14 @@
 
     own_copy = pltpu.make_async_copy(bsend.at[band], out_ref.at[band], own_sem)
     own_copy.start()
+
+    fill = jnp.zeros((FPAD - nfld, ndeg), F32)
+    for s in range(slots):
+        loaded = spec_ref[s].astype(F32)
+        components = [jnp.concatenate([loaded[:, c, :], fill], axis=0).astype(BF16) for c in range(2)]
+        values_v[s] = jnp.concatenate(components, axis=0)
+    values_copy = pltpu.make_async_copy(values_v, values_hbm, values_sem)
+    values_copy.start()
     own_copy.wait()
     values_copy.wait()
     pltpu.make_async_copy(out_ref.at[pl.ds(0, nb - 1)], out_ref.at[pl.ds(0, nb - 1)], recv_sem.at[3]).wait()

time: 67.8 us -> 66.6 us (0.982)
  Pallas kernels: 67.6 us -> 66.4 us
    pallas_call x1, Pallas kernels: 61.8 us -> 60.6 us  [shards(): pl.pallas_call(functools.partial(round_kernel, nb, nl), out_shape=(jax.Sh...]
where the time goes in v2:
time: 66.6 us; the launch traced here: 66.4 us
  Pallas kernels  66.4 us (100%)
    pallas_call x1, Pallas kernels, shards(): pl.pallas_call(functools.partial(round_kernel, nb, nl), out_shape=(jax.Sh...  60.6 us
    pallas_call x1, Pallas kernels, shards(): pl.pallas_call(functools.partial(update_kernel, nb), out_shape=jax.ShapeD...  5.81 us

profile of v2, /device:TPU:1, one launch (start us, length us, event | category | flops | bytes accessed | tf_op | source)
XLA Modules:
  0.0 66.4 jit_solution(342047344954616690)
XLA Ops:
  0.0 60.6 %shard_map.73 = (bf16[96,8,128]{2,1,0:T(8,128)(2,1)}, bf16[14,32,1280]{2,1,0:T(8,128)(2,1)}) custom-call(s32[1344]{0:T(1024)} %wave_s.3, s32[192]{0:T(256)} %points_s.1, f32[192]{0:T(256)} %gauss_s.1, f32[24]{0:T(128)} %layer_s.1, bf16[14,15,2,1280]{3,2,1,0:T(2,128)(2,1)} %bitcast.11, bf16[14,192,1280]{2,1,0:T(8,128)(2,1)} %bitcast.9), custom_call_target="tpu_custom_call" | custom-call | tf_op jit(solution)/shard_map/pallas_call | solution.py:530
  60.6 5.8 %shard_map.74 = f32[4200,128]{1,0:T(8,128)} custom-call(s32[1344]{0:T(1024)} %wave_s.3, f32[15]{0:T(128)} %speed_s.1, bf16[96,8,128]{2,1,0:T(8,128)(2,1)} %get-tuple-element.7.arrived_hbm, bf16[14,32,1280]{2,1,0:T(8,128)(2,1)} %get-tuple-element.8.values_hbm, bf16[14,192,1280]{2,1,0:T(8,128)(2,1)} %bitcast.10), custom_call_target="tpu_custom_call" | custom-call | tf_op jit(solution)/shard_map/pallas_call | solution.py:578
